TPU v7x, 256 devices: a whole 4x4x8 slice. The times are simulated.
256 devices in a mesh: term: 8 (over z), sec: 32 (over y, x, core).
Axes of the slice: x: 4, y: 4, z: 8, core: 2. Of those that a mesh axis runs over, the one named last changes fastest.
Arguments:
- start_vectors: bfloat16 [2, 64, 256, 256], P(None, 'sec'), may hold values from -6 to 6
- left_env: bfloat16 [32, 64, 256, 256], P('term', 'sec'), may hold values from -0.375 to 0.375
- right_env: bfloat16 [32, 64, 256, 256], P('term', 'sec'), may hold values from -0.375 to 0.375
- term_shift: int32 [32], P('term'), may hold values from -1 to 1
- precond: float32 [64, 256, 256], P('sec'), may hold values from 0.25 to 4
- block_dims: int32 [64], P('sec'), may hold values from 1 to 256, 8192 in all
Outputs:
- vector: float32 [2, 64, 256, 256], P(None, 'sec', 'term')
- energy: float32 [2], replicated
Inputs may be any that keep to these rules, and one draw needn't show every extreme that they name: `block_dims`: one block has exactly 256 live states.
All inputs are finite; a program needn't handle non-finite values.
Results may differ from a plain program's by a relative error of at most 0.0036.
Values may be sent and summed in bfloat16 or wider, within the bound.
No kernel may reach another device: no remote copies, remote signals or barrier semaphores. Data moves between devices by JAX's collectives and lax.ppermute only.
A program may use at most 64 MiB of HBM per device.

v0:
```python
import jax
import jax.numpy as jnp
from jax import lax
from jax.sharding import PartitionSpec as P

ITERS = 2


def padded(x, sides, width):
    for axis, dim in sides:
        count, length = (lax.axis_size(axis), x.shape[dim])
        up = [(i, (i + 1) % count) for i in range(count - 1)]
        down = [(j, i) for i, j in up]
        last = lax.slice_in_dim(x, length - width, length, axis=dim)
        initial = lax.slice_in_dim(x, 0, width, axis=dim)
        before = lax.ppermute(last, axis, up)
        after = lax.ppermute(initial, axis, down)
        x = jnp.concatenate([before, x, after], axis=dim)
    return x


def shards(start_vectors, left_env, right_env, term_shift, precond, block_dims):
    vec_count, blocks, states, _ = start_vectors.shape
    groups = lax.axis_size("term")
    share = states // groups
    offset_row = lax.axis_index("term") * share
    factor = 1.0 / (blocks * lax.axis_size("sec") * states * states)
    position = jnp.arange(states, dtype=jnp.int32)
    live_rows = position[None, :, None] < block_dims[:, None, None]
    live_cols = position[None, None, :] < block_dims[:, None, None]
    mask = (live_rows & live_cols).astype(jnp.float32)
    shift_sel = term_shift[:, None, None, None, None]

    def apply_op(vector_bf):
        local = jnp.einsum(
            "ujab,kjcb->kujac", vector_bf, right_env, preferred_element_type=jnp.float32
        ).astype(jnp.bfloat16)
        wide = padded(local, (("sec", 2),), 1)
        chosen = jnp.where(
            shift_sel < 0,
            wide[:, :, 0:blocks],
            jnp.where(shift_sel == 0, wide[:, :, 1 : blocks + 1], wide[:, :, 2 : blocks + 2]),
        )
        partial_sum = (
            jnp.einsum("kbac,kubcd->ubad", left_env, chosen, preferred_element_type=jnp.float32)
            * mask
        )
        result = lax.psum(partial_sum, "term")
        return result

    def totals(values):
        result = lax.psum(values, "sec")
        return result

    def inner(left, right):
        return jnp.sum(left * right, axis=(1, 2, 3)) * factor

    def expand(value):
        return value[:, None, None, None]

    start = start_vectors * mask.astype(jnp.bfloat16)
    h_vec = apply_op(start)
    vector = start.astype(jnp.float32)
    pre_view = precond[None]
    length = jnp.sqrt(totals(inner(vector, vector)[None])[0] + 1e-06)
    vector = vector / expand(length)
    h_vec = h_vec / expand(length)
    energy = jnp.zeros((vec_count,), jnp.float32)
    for iteration in range(ITERS):
        rayleigh = totals(inner(vector, h_vec)[None])[0]
        resid = h_vec - expand(rayleigh) * vector
        precon_res = pre_view * resid
        correlation = totals(inner(vector, precon_res)[None])[0]
        direction = precon_res - expand(correlation) * vector
        pair = totals(jnp.stack([inner(direction, direction), inner(direction, h_vec)]))
        square, raw_coupling = (pair[0], pair[1])
        dir_norm = jnp.sqrt(square + 1e-06)
        coupling = raw_coupling / dir_norm
        direction = direction / expand(dir_norm)
        widen_result = direction.astype(jnp.bfloat16)
        h_dir = apply_op(widen_result)
        curvature = totals(inner(direction, h_dir)[None])[0]
        energy = 0.5 * (rayleigh + curvature) - jnp.sqrt(
            (0.5 * (rayleigh - curvature)) ** 2 + coupling**2
        )
        weight = energy - rayleigh
        new_size = jnp.sqrt(coupling**2 + weight**2)
        vector = (expand(coupling) * vector + expand(weight) * direction) / expand(new_size)
        h_vec = (expand(coupling) * h_vec + expand(weight) * h_dir) / expand(new_size)
    final = lax.dynamic_slice_in_dim(vector, offset_row, share, 2)
    return (final, energy)


def solution(mesh):
    return jax.shard_map(
        shards,
        mesh=mesh,
        in_specs=(
            P(None, "sec", None, None),
            P("term", "sec", None, None),
            P("term", "sec", None, None),
            P("term"),
            P("sec", None, None),
            P("sec"),
        ),
        out_specs=(P(None, "sec", "term", None), P()),
        check_vma=False,
    )
```

profile of v0, /device:TPU:1, one launch (start us, length us, event | category | flops | bytes accessed | tf_op | source)
XLA Modules:
  0.0 827.7 jit_solution(5210906045877564215)
XLA Ops:
  10.7 4.6 collective-permute-start
  15.3 2.0 collective-permute-start.1
  17.3 9.7 %collective-permute-done = bf16[4,2,1,256,256]{4,3,0,1,2:T(8,128)(2,1)S(1)} collective-permute-done((bf16[4,2,1,256,256]{4,3,0,1,2:T(8,128)(2,1)S(1)}, bf16[4,2,1,256,256]{4,3,0,1,2:T(8,128)(2,1)S(1)}, u32[]{:S(2)}, u32[]{:S(2)}) %collective-permute-start) | collective-permute-done | bytes 1048608 | tf_op jit(solution)/shard_map/ppermute | solution.py:16
  27.1 4.4 collective-permute-done.1
  31.5 2.4 fusion.27
  34.3 61.0 %psum.85 = f32[1,2]{1,0:T(1,128)S(1)} all-reduce(f32[1,2]{1,0:T(1,128)S(1)} %multiply_bitcast_fusion.6), channel_id=1, replica_groups=mesh['term'=8,'sec'=32] {'sec'}, use_global_device_ids=true, to_apply=%region_2.3 | all-reduce | flops 2 | bytes 16 | tf_op jit(solution)/shard_map/psum | solution.py:52
  95.3 14.4 %all-reduce.4.cloned.1.call-done = f32[2,2,256,256]{2,3,0,1:T(8,128)} async-done(((f32[2,2,256,256]{2,3,0,1:T(8,128)}), f32[2,2,256,256]{2,3,0,1:T(8,128)}) %all-reduce.4.cloned.1.call-update) | async-done | bytes 1048592 | tf_op jit(solution)/shard_map/psum | solution.py:48
  112.6 67.1 %psum.86 = f32[2]{0:T(128)S(1)} all-reduce(f32[2]{0:T(128)S(1)} %broadcast_multiply_fusion.5), channel_id=1, replica_groups=mesh['term'=8,'sec'=32] {'sec'}, use_global_device_ids=true, to_apply=%region_4.5 | all-reduce | flops 2 | bytes 16 | tf_op jit(solution)/shard_map/psum | solution.py:52
  180.2 62.7 %psum.87 = f32[2]{0:T(128)S(1)} all-reduce(f32[2]{0:T(128)S(1)} %broadcast_multiply_fusion.4), channel_id=1, replica_groups=mesh['term'=8,'sec'=32] {'sec'}, use_global_device_ids=true, to_apply=%region_6.7 | all-reduce | flops 2 | bytes 16 | tf_op jit(solution)/shard_map/psum | solution.py:52
  244.5 62.7 %psum.88 = f32[2,2]{1,0:T(2,128)S(1)} all-reduce(f32[2,2]{1,0:T(2,128)S(1)} %pad_maximum_fusion.9), channel_id=1, replica_groups=mesh['term'=8,'sec'=32] {'sec'}, use_global_device_ids=true, to_apply=%region_9.10 | all-reduce | flops 4 | bytes 32 | tf_op jit(solution)/shard_map/psum | solution.py:52
  307.2 2.1 convert_bitcast_fusion.1
  309.5 2.1 collective-permute-start.2
  311.6 2.5 collective-permute-start.3
  314.0 9.2 %collective-permute-done.2 = bf16[4,2,1,256,256]{4,3,0,1,2:T(8,128)(2,1)S(1)} collective-permute-done((bf16[4,2,1,256,256]{4,3,0,1,2:T(8,128)(2,1)S(1)}, bf16[4,2,1,256,256]{4,3,0,1,2:T(8,128)(2,1)S(1)}, u32[]{:S(2)}, u32[]{:S(2)}) %collective-permute-start.2) | collective-permute-done | bytes 1048608 | tf_op jit(solution)/shard_map/ppermute | solution.py:16
  323.3 4.4 collective-permute-done.3
  327.7 2.4 fusion.33
  330.1 65.6 %all-reduce.6.cloned.1.call-done = f32[2,2,256,256]{2,3,0,1:T(8,128)} async-done(((f32[2,2,256,256]{2,3,0,1:T(8,128)}), f32[2,2,256,256]{2,3,0,1:T(8,128)}) %all-reduce.6.cloned.1.call-update) | async-done | bytes 1048592 | tf_op jit(solution)/shard_map/psum | solution.py:48
  397.7 67.1 %psum.90 = f32[2]{0:T(128)S(1)} all-reduce(f32[2]{0:T(128)S(1)} %broadcast_multiply_fusion.3), channel_id=1, replica_groups=mesh['term'=8,'sec'=32] {'sec'}, use_global_device_ids=true, to_apply=%region_12.13 | all-reduce | flops 2 | bytes 16 | tf_op jit(solution)/shard_map/psum | solution.py:52
  464.8 3.5 multiply_reduce_fusion.4
  468.3 62.8 %psum.91 = f32[2]{0:T(128)S(1)} all-reduce(f32[2]{0:T(128)S(1)} %broadcast_multiply_fusion.2), channel_id=1, replica_groups=mesh['term'=8,'sec'=32] {'sec'}, use_global_device_ids=true, to_apply=%region_14.15 | all-reduce | flops 2 | bytes 16 | tf_op jit(solution)/shard_map/psum | solution.py:52
  531.1 1.9 multiply_reduce_fusion.3
  533.0 62.7 %psum.92 = f32[2]{0:T(128)S(1)} all-reduce(f32[2]{0:T(128)S(1)} %broadcast_multiply_fusion.1), channel_id=1, replica_groups=mesh['term'=8,'sec'=32] {'sec'}, use_global_device_ids=true, to_apply=%region_16.17 | all-reduce | flops 2 | bytes 16 | tf_op jit(solution)/shard_map/psum | solution.py:52
  595.6 2.6 multiply_reduce_fusion.2
  598.2 62.7 %psum.93 = f32[2,2]{1,0:T(2,128)S(1)} all-reduce(f32[2,2]{1,0:T(2,128)S(1)} %pad_maximum_fusion.10), channel_id=1, replica_groups=mesh['term'=8,'sec'=32] {'sec'}, use_global_device_ids=true, to_apply=%region_19.20 | all-reduce | flops 4 | bytes 32 | tf_op jit(solution)/shard_map/psum | solution.py:52
  663.5 2.1 collective-permute-start.4
  665.6 2.5 collective-permute-start.5
  668.1 9.2 %collective-permute-done.4 = bf16[4,2,1,256,256]{4,3,0,1,2:T(8,128)(2,1)S(1)} collective-permute-done((bf16[4,2,1,256,256]{4,3,0,1,2:T(8,128)(2,1)S(1)}, bf16[4,2,1,256,256]{4,3,0,1,2:T(8,128)(2,1)S(1)}, u32[]{:S(2)}, u32[]{:S(2)}) %collective-permute-start.4) | collective-permute-done | bytes 1048608 | tf_op jit(solution)/shard_map/ppermute | solution.py:16
  677.3 4.4 collective-permute-done.5
  681.7 2.4 fusion.39
  684.1 65.3 %all-reduce.8.cloned.1.call-done = f32[2,2,256,256]{2,3,0,1:T(8,128)} async-done(((f32[2,2,256,256]{2,3,0,1:T(8,128)}), f32[2,2,256,256]{2,3,0,1:T(8,128)}) %all-reduce.8.cloned.1.call-update) | async-done | bytes 1048592 | tf_op jit(solution)/shard_map/psum | solution.py:48
  749.4 1.9 multiply_reduce_fusion
  751.3 67.1 %psum.95 = f32[2]{0:T(128)S(1)} all-reduce(f32[2]{0:T(128)S(1)} %broadcast_multiply_fusion), channel_id=1, replica_groups=mesh['term'=8,'sec'=32] {'sec'}, use_global_device_ids=true, to_apply=%region_22.23 | all-reduce | flops 2 | bytes 16 | tf_op jit(solution)/shard_map/psum | solution.py:52
  (63 shorter events, 16.4 us)
Async XLA Ops:
  7.2 2.5 copy-start
  7.2 102.5 %all-reduce.4.cloned.1.call-start = ((), (), s32[]{:S(2)}) async-start(), calls=%async_computation | async-start | bytes 2097152 | tf_op jit(solution)/shard_map/psum | solution.py:48
  8.2 23.3 %copy-start.4 = (f32[2,256,256]{1,2,0:T(8,128)}, f32[2,256,256]{1,2,0:T(8,128)S(1)}, u32[]{:S(2)}) copy-start(f32[2,256,256]{1,2,0:T(8,128)S(1)} %get-tuple-element.26) | copy-start | bytes 1572868
  10.5 6.8 copy-start.10
  10.5 21.0 %copy-start.7 = (bf16[4,2,256,256]{3,2,1,0:T(8,128)(2,1)S(1)}, bf16[4,2,256,256]{3,2,1,0:T(8,128)(2,1)}, u32[]{:S(2)}) copy-start(bf16[4,2,256,256]{3,2,1,0:T(8,128)(2,1)} %param.7) | copy-start | bytes 3145732
  10.7 16.4 %collective-permute-start = (bf16[4,2,1,256,256]{4,3,0,1,2:T(8,128)(2,1)S(1)}, bf16[4,2,1,256,256]{4,3,0,1,2:T(8,128)(2,1)S(1)}, u32[]{:S(2)}, u32[]{:S(2)}) collective-permute-start(bf16[4,2,1,256,256]{4,3,0,1,2:T(8,128)(2,1)S(1)} %get-tuple-element.24), channel_id=1, source_target_pairs={{0,1},{1,2},{2,3},{3,4},{4,5},{5,6},{6,7},{7,8},{8,9},{9,10},{10,1... | collective-permute-start | bytes 3145736 | tf_op jit(solution)/shard_map/ppermute | solution.py:16
  15.3 16.1 %collective-permute-start.1 = (bf16[4,2,1,256,256]{4,3,0,1,2:T(8,128)(2,1)S(1)}, bf16[4,2,1,256,256]{4,3,0,1,2:T(8,128)(2,1)S(1)}, u32[]{:S(2)}, u32[]{:S(2)}) collective-permute-start(bf16[4,2,1,256,256]{4,3,0,1,2:T(8,128)(2,1)S(1)} %get-tuple-element.25), channel_id=1, source_target_pairs={{1,0},{2,1},{3,2},{4,3},{5,4},{6,5},{7,6},{8,7},{9,8},{10,9},{11,1... | collective-permute-start | bytes 3145736 | tf_op jit(solution)/shard_map/ppermute | solution.py:17
  33.9 361.9 %all-reduce.6.cloned.1.call-start = ((), (), s32[]{:S(2)}) async-start(), calls=%async_computation.1 | async-start | bytes 2097152 | tf_op jit(solution)/shard_map/psum | solution.py:48
  109.7 70.1 %copy-start.1 = (f32[2,2,256,256]{2,3,0,1:T(8,128)S(1)}, f32[2,2,256,256]{2,3,0,1:T(8,128)}, u32[]{:S(2)}) copy-start(f32[2,2,256,256]{2,3,0,1:T(8,128)} %all-reduce.4.cloned.1.call-done) | copy-start | bytes 3145732
  309.3 18.4 %copy-start.5 = (f32[2,256,256]{1,2,0:T(8,128)S(1)}, f32[2,256,256]{1,2,0:T(8,128)}, u32[]{:S(2)}) copy-start(f32[2,256,256]{1,2,0:T(8,128)} %copy-done.4) | copy-start | bytes 1572868
  309.3 18.4 %copy-start.8 = (bf16[4,2,256,256]{3,2,1,0:T(8,128)(2,1)S(1)}, bf16[4,2,256,256]{3,2,1,0:T(8,128)(2,1)}, u32[]{:S(2)}) copy-start(bf16[4,2,256,256]{3,2,1,0:T(8,128)(2,1)} %param.7) | copy-start | bytes 3145732
  309.5 13.8 %collective-permute-start.2 = (bf16[4,2,1,256,256]{4,3,0,1,2:T(8,128)(2,1)S(1)}, bf16[4,2,1,256,256]{4,3,0,1,2:T(8,128)(2,1)S(1)}, u32[]{:S(2)}, u32[]{:S(2)}) collective-permute-start(bf16[4,2,1,256,256]{4,3,0,1,2:T(8,128)(2,1)S(1)} %get-tuple-element.22), channel_id=1, source_target_pairs={{0,1},{1,2},{2,3},{3,4},{4,5},{5,6},{6,7},{7,8},{8,9},{9,10},{10,1... | collective-permute-start | bytes 3145736 | tf_op jit(solution)/shard_map/ppermute | solution.py:16
  311.6 16.1 %collective-permute-start.3 = (bf16[4,2,1,256,256]{4,3,0,1,2:T(8,128)(2,1)S(1)}, bf16[4,2,1,256,256]{4,3,0,1,2:T(8,128)(2,1)S(1)}, u32[]{:S(2)}, u32[]{:S(2)}) collective-permute-start(bf16[4,2,1,256,256]{4,3,0,1,2:T(8,128)(2,1)S(1)} %get-tuple-element.23), channel_id=1, source_target_pairs={{1,0},{2,1},{3,2},{4,3},{5,4},{6,5},{7,6},{8,7},{9,8},{10,9},{11,1... | collective-permute-start | bytes 3145736 | tf_op jit(solution)/shard_map/ppermute | solution.py:17
  330.1 419.3 %all-reduce.8.cloned.1.call-start = ((), (), s32[]{:S(2)}) async-start(), calls=%async_computation.2 | async-start | bytes 2097152 | tf_op jit(solution)/shard_map/psum | solution.py:48
  468.3 127.4 %copy-start.2 = (f32[2,2,256,256]{2,3,0,1:T(8,128)S(1)}, f32[2,2,256,256]{2,3,0,1:T(8,128)}, u32[]{:S(2)}) copy-start(f32[2,2,256,256]{2,3,0,1:T(8,128)} %get-tuple-element.15) | copy-start | bytes 3145732
  662.3 1.0 copy-start.3
  663.4 18.4 %copy-start.6 = (f32[2,256,256]{1,2,0:T(8,128)S(1)}, f32[2,256,256]{1,2,0:T(8,128)}, u32[]{:S(2)}) copy-start(f32[2,256,256]{1,2,0:T(8,128)} %copy-done.4) | copy-start | bytes 1572868
  663.4 18.4 %copy-start.9 = (bf16[4,2,256,256]{3,2,1,0:T(8,128)(2,1)S(1)}, bf16[4,2,256,256]{3,2,1,0:T(8,128)(2,1)}, u32[]{:S(2)}) copy-start(bf16[4,2,256,256]{3,2,1,0:T(8,128)(2,1)} %param.7) | copy-start | bytes 3145732
  663.5 13.8 %collective-permute-start.4 = (bf16[4,2,1,256,256]{4,3,0,1,2:T(8,128)(2,1)S(1)}, bf16[4,2,1,256,256]{4,3,0,1,2:T(8,128)(2,1)S(1)}, u32[]{:S(2)}, u32[]{:S(2)}) collective-permute-start(bf16[4,2,1,256,256]{4,3,0,1,2:T(8,128)(2,1)S(1)} %get-tuple-element.20), channel_id=1, source_target_pairs={{0,1},{1,2},{2,3},{3,4},{4,5},{5,6},{6,7},{7,8},{8,9},{9,10},{10,1... | collective-permute-start | bytes 3145736 | tf_op jit(solution)/shard_map/ppermute | solution.py:16
  665.6 16.1 %collective-permute-start.5 = (bf16[4,2,1,256,256]{4,3,0,1,2:T(8,128)(2,1)S(1)}, bf16[4,2,1,256,256]{4,3,0,1,2:T(8,128)(2,1)S(1)}, u32[]{:S(2)}, u32[]{:S(2)}) collective-permute-start(bf16[4,2,1,256,256]{4,3,0,1,2:T(8,128)(2,1)S(1)} %get-tuple-element.21), channel_id=1, source_target_pairs={{1,0},{2,1},{3,2},{4,3},{5,4},{6,5},{7,6},{8,7},{9,8},{10,9},{11,1... | collective-permute-start | bytes 3145736 | tf_op jit(solution)/shard_map/ppermute | solution.py:17
Sparse Core Ops, SparseCore 0:
  34.0 75.5 all-reduce.3
  330.2 65.5 all-reduce.5
  684.2 65.1 all-reduce.7
where the time goes:
time: 829 us; the launch traced here: 828 us
  blocking collectives  576 us (69%)
  waiting for transfers between devices  187 us (23%)
  other arithmetic  20.1 us (2%)
  starting transfers between devices  15.8 us (2%)
  between operations  14 us (2%)
  matrix products  11 us (1%)
    psum x9, blocking collectives, totals(): result = lax.psum(values, 'sec')  576 us
    psum x3, waiting for transfers between devices, apply_op(): result = lax.psum(partial_sum, 'term')  145 us
    ppermute x3, waiting for transfers between devices, padded(): before = lax.ppermute(last, axis, up)  28.2 us
  transfers between devices with their start and end apart: 9, of which 9 were waited for; matrix products, arithmetic and copies ran while one was open for 0% of the time, Pallas kernels for 0%

commit v1 on v0

--- a/solution.py
+++ b/solution.py
@@ -45,7 +45,7 @@
             jnp.einsum("kbac,kubcd->ubad", left_env, chosen, preferred_element_type=jnp.float32)
             * mask
         )
-        result = lax.psum(partial_sum, "term")
+        result = jnp.sum(lax.all_gather(partial_sum, "term"), axis=0)
         return result
 
     def totals(values):

time: 829 us -> 906 us (1.093)
  waiting for transfers between devices: 187 us -> 253 us
  other arithmetic: 20.1 us -> 33.1 us
    all_gather x0 -> x3, waiting for transfers between devices: none -> 212 us  [apply_op(): result = jnp.sum(lax.all_gather(partial_sum, 'term'), axis=0)]
    psum x3 -> x0, waiting for transfers between devices: 145 us -> none  [apply_op(): result = lax.psum(partial_sum, 'term')]
    reduce_sum x0 -> x3, other arithmetic: none -> 14.1 us  [apply_op(): result = jnp.sum(lax.all_gather(partial_sum, 'term'), axis=0)]
where the time goes in v1:
time: 906 us; the launch traced here: 903 us
  blocking collectives  571 us (63%)
  waiting for transfers between devices  253 us (28%)
  other arithmetic  33.1 us (4%)
  starting transfers between devices  15.8 us (2%)
  between operations  14 us (2%)
  matrix products  11.1 us (1%)
    psum x9, blocking collectives, totals(): result = lax.psum(values, 'sec')  571 us
    all_gather x3, waiting for transfers between devices, apply_op(): result = jnp.sum(lax.all_gather(partial_sum, 'term'), axis=0)  212 us
    ppermute x3, waiting for transfers between devices, padded(): before = lax.ppermute(last, axis, up)  28.2 us
  transfers between devices with their start and end apart: 9, of which 9 were waited for; matrix products, arithmetic and copies ran while one was open for 0% of the time, Pallas kernels for 0%

profile of v1, /device:TPU:1, one launch (start us, length us, event | category | flops | bytes accessed | tf_op | source)
XLA Modules:
  0.0 903.1 jit_solution(5213167288452984919)
XLA Ops:
  10.7 4.6 collective-permute-start
  17.3 9.7 %collective-permute-done = bf16[4,2,1,256,256]{4,3,0,1,2:T(8,128)(2,1)S(1)} collective-permute-done((bf16[4,2,1,256,256]{4,3,0,1,2:T(8,128)(2,1)S(1)}, bf16[4,2,1,256,256]{4,3,0,1,2:T(8,128)(2,1)S(1)}, u32[]{:S(2)}, u32[]{:S(2)}) %collective-permute-start) | collective-permute-done | bytes 1048608 | tf_op jit(solution)/shard_map/ppermute | solution.py:16
  27.1 4.4 collective-permute-done.1
  31.5 2.5 fusion.27
  34.3 61.0 %psum.63 = f32[1,2]{1,0:T(1,128)S(1)} all-reduce(f32[1,2]{1,0:T(1,128)S(1)} %multiply_bitcast_fusion.6), channel_id=1, replica_groups=mesh['term'=8,'sec'=32] {'sec'}, use_global_device_ids=true, to_apply=%region_2.3 | all-reduce | flops 2 | bytes 16 | tf_op jit(solution)/shard_map/psum | solution.py:52
  95.3 36.7 %all-gather.7.cloned.1.call-done = f32[16,2,256,256]{2,3,0,1:T(8,128)} async-done(((f32[2,2,256,256]{2,3,0,1:T(8,128)}), f32[16,2,256,256]{2,3,0,1:T(8,128)}) %all-gather.7.cloned.1.call-update) | async-done | bytes 8388624 | tf_op jit(solution)/shard_map/all_gather | solution.py:48
  132.0 4.1 reduce_sum.126
  137.7 62.9 %psum.64 = f32[2]{0:T(128)S(1)} all-reduce(f32[2]{0:T(128)S(1)} %broadcast_multiply_fusion.5), channel_id=1, replica_groups=mesh['term'=8,'sec'=32] {'sec'}, use_global_device_ids=true, to_apply=%region_4.5 | all-reduce | flops 2 | bytes 16 | tf_op jit(solution)/shard_map/psum | solution.py:52
  201.1 66.8 %psum.65 = f32[2]{0:T(128)S(1)} all-reduce(f32[2]{0:T(128)S(1)} %broadcast_multiply_fusion.4), channel_id=1, replica_groups=mesh['term'=8,'sec'=32] {'sec'}, use_global_device_ids=true, to_apply=%region_6.7 | all-reduce | flops 2 | bytes 16 | tf_op jit(solution)/shard_map/psum | solution.py:52
  269.5 62.7 %psum.66 = f32[2,2]{1,0:T(2,128)S(1)} all-reduce(f32[2,2]{1,0:T(2,128)S(1)} %pad_maximum_fusion.9), channel_id=1, replica_groups=mesh['term'=8,'sec'=32] {'sec'}, use_global_device_ids=true, to_apply=%region_9.10 | all-reduce | flops 4 | bytes 32 | tf_op jit(solution)/shard_map/psum | solution.py:52
  332.2 2.1 convert_bitcast_fusion.1
  334.6 2.1 collective-permute-start.2
  336.6 2.5 collective-permute-start.3
  339.1 9.2 %collective-permute-done.2 = bf16[4,2,1,256,256]{4,3,0,1,2:T(8,128)(2,1)S(1)} collective-permute-done((bf16[4,2,1,256,256]{4,3,0,1,2:T(8,128)(2,1)S(1)}, bf16[4,2,1,256,256]{4,3,0,1,2:T(8,128)(2,1)S(1)}, u32[]{:S(2)}, u32[]{:S(2)}) %collective-permute-start.2) | collective-permute-done | bytes 1048608 | tf_op jit(solution)/shard_map/ppermute | solution.py:16
  348.4 4.4 collective-permute-done.3
  352.8 2.4 fusion.33
  355.2 87.7 %all-gather.9.cloned.1.call-done = f32[16,2,256,256]{2,3,0,1:T(8,128)} async-done(((f32[2,2,256,256]{2,3,0,1:T(8,128)}), f32[16,2,256,256]{2,3,0,1:T(8,128)}) %all-gather.9.cloned.1.call-update) | async-done | bytes 8388624 | tf_op jit(solution)/shard_map/all_gather | solution.py:48
  442.9 5.0 reduce_sum.132
  449.8 62.9 %psum.67 = f32[2]{0:T(128)S(1)} all-reduce(f32[2]{0:T(128)S(1)} %broadcast_multiply_fusion.3), channel_id=1, replica_groups=mesh['term'=8,'sec'=32] {'sec'}, use_global_device_ids=true, to_apply=%region_12.13 | all-reduce | flops 2 | bytes 16 | tf_op jit(solution)/shard_map/psum | solution.py:52
  512.7 3.5 multiply_reduce_fusion.4
  516.1 66.9 %psum.68 = f32[2]{0:T(128)S(1)} all-reduce(f32[2]{0:T(128)S(1)} %broadcast_multiply_fusion.2), channel_id=1, replica_groups=mesh['term'=8,'sec'=32] {'sec'}, use_global_device_ids=true, to_apply=%region_14.15 | all-reduce | flops 2 | bytes 16 | tf_op jit(solution)/shard_map/psum | solution.py:52
  585.0 62.7 %psum.69 = f32[2]{0:T(128)S(1)} all-reduce(f32[2]{0:T(128)S(1)} %broadcast_multiply_fusion.1), channel_id=1, replica_groups=mesh['term'=8,'sec'=32] {'sec'}, use_global_device_ids=true, to_apply=%region_16.17 | all-reduce | flops 2 | bytes 16 | tf_op jit(solution)/shard_map/psum | solution.py:52
  647.6 2.6 multiply_reduce_fusion.2
  650.3 62.9 %psum.70 = f32[2,2]{1,0:T(2,128)S(1)} all-reduce(f32[2,2]{1,0:T(2,128)S(1)} %pad_maximum_fusion.10), channel_id=1, replica_groups=mesh['term'=8,'sec'=32] {'sec'}, use_global_device_ids=true, to_apply=%region_19.20 | all-reduce | flops 4 | bytes 32 | tf_op jit(solution)/shard_map/psum | solution.py:52
  715.7 2.1 collective-permute-start.4
  717.8 2.5 collective-permute-start.5
  720.3 9.2 %collective-permute-done.4 = bf16[4,2,1,256,256]{4,3,0,1,2:T(8,128)(2,1)S(1)} collective-permute-done((bf16[4,2,1,256,256]{4,3,0,1,2:T(8,128)(2,1)S(1)}, bf16[4,2,1,256,256]{4,3,0,1,2:T(8,128)(2,1)S(1)}, u32[]{:S(2)}, u32[]{:S(2)}) %collective-permute-start.4) | collective-permute-done | bytes 1048608 | tf_op jit(solution)/shard_map/ppermute | solution.py:16
  729.5 4.4 collective-permute-done.5
  733.9 2.4 fusion.39
  736.3 87.7 %all-gather.11.cloned.1.call-done = f32[16,2,256,256]{2,3,0,1:T(8,128)} async-done(((f32[2,2,256,256]{2,3,0,1:T(8,128)}), f32[16,2,256,256]{2,3,0,1:T(8,128)}) %all-gather.11.cloned.1.call-update) | async-done | bytes 8388624 | tf_op jit(solution)/shard_map/all_gather | solution.py:48
  824.0 5.0 reduce_sum.138
  830.9 62.9 %psum.71 = f32[2]{0:T(128)S(1)} all-reduce(f32[2]{0:T(128)S(1)} %broadcast_multiply_fusion), channel_id=1, replica_groups=mesh['term'=8,'sec'=32] {'sec'}, use_global_device_ids=true, to_apply=%region_22.23 | all-reduce | flops 2 | bytes 16 | tf_op jit(solution)/shard_map/psum | solution.py:52
  (64 shorter events, 20.9 us)
Async XLA Ops:
  7.2 2.5 copy-start
  7.2 124.8 %all-gather.7.cloned.1.call-start = ((), (), s32[]{:S(2)}) async-start(), calls=%async_computation | async-start | bytes 9437184 | tf_op jit(solution)/shard_map/all_gather | solution.py:48
  8.2 23.3 %copy-start.3 = (f32[2,256,256]{1,2,0:T(8,128)}, f32[2,256,256]{1,2,0:T(8,128)S(1)}, u32[]{:S(2)}) copy-start(f32[2,256,256]{1,2,0:T(8,128)S(1)} %get-tuple-element.26) | copy-start | bytes 1572868
  10.5 6.8 copy-start.9
  10.5 21.0 %copy-start.6 = (bf16[4,2,256,256]{3,2,1,0:T(8,128)(2,1)S(1)}, bf16[4,2,256,256]{3,2,1,0:T(8,128)(2,1)}, u32[]{:S(2)}) copy-start(bf16[4,2,256,256]{3,2,1,0:T(8,128)(2,1)} %param.7) | copy-start | bytes 3145732
  10.7 16.4 %collective-permute-start = (bf16[4,2,1,256,256]{4,3,0,1,2:T(8,128)(2,1)S(1)}, bf16[4,2,1,256,256]{4,3,0,1,2:T(8,128)(2,1)S(1)}, u32[]{:S(2)}, u32[]{:S(2)}) collective-permute-start(bf16[4,2,1,256,256]{4,3,0,1,2:T(8,128)(2,1)S(1)} %get-tuple-element.24), channel_id=1, source_target_pairs={{0,1},{1,2},{2,3},{3,4},{4,5},{5,6},{6,7},{7,8},{8,9},{9,10},{10,1... | collective-permute-start | bytes 3145736 | tf_op jit(solution)/shard_map/ppermute | solution.py:16
  15.3 16.1 %collective-permute-start.1 = (bf16[4,2,1,256,256]{4,3,0,1,2:T(8,128)(2,1)S(1)}, bf16[4,2,1,256,256]{4,3,0,1,2:T(8,128)(2,1)S(1)}, u32[]{:S(2)}, u32[]{:S(2)}) collective-permute-start(bf16[4,2,1,256,256]{4,3,0,1,2:T(8,128)(2,1)S(1)} %get-tuple-element.25), channel_id=1, source_target_pairs={{1,0},{2,1},{3,2},{4,3},{5,4},{6,5},{7,6},{8,7},{9,8},{10,9},{11,1... | collective-permute-start | bytes 3145736 | tf_op jit(solution)/shard_map/ppermute | solution.py:17
  33.9 408.9 %all-gather.9.cloned.1.call-start = ((), (), s32[]{:S(2)}) async-start(), calls=%async_computation.1 | async-start | bytes 9437184 | tf_op jit(solution)/shard_map/all_gather | solution.py:48
  334.4 18.4 %copy-start.4 = (f32[2,256,256]{1,2,0:T(8,128)S(1)}, f32[2,256,256]{1,2,0:T(8,128)}, u32[]{:S(2)}) copy-start(f32[2,256,256]{1,2,0:T(8,128)} %copy-done.3) | copy-start | bytes 1572868
  334.4 18.4 %copy-start.7 = (bf16[4,2,256,256]{3,2,1,0:T(8,128)(2,1)S(1)}, bf16[4,2,256,256]{3,2,1,0:T(8,128)(2,1)}, u32[]{:S(2)}) copy-start(bf16[4,2,256,256]{3,2,1,0:T(8,128)(2,1)} %param.7) | copy-start | bytes 3145732
  334.6 13.8 %collective-permute-start.2 = (bf16[4,2,1,256,256]{4,3,0,1,2:T(8,128)(2,1)S(1)}, bf16[4,2,1,256,256]{4,3,0,1,2:T(8,128)(2,1)S(1)}, u32[]{:S(2)}, u32[]{:S(2)}) collective-permute-start(bf16[4,2,1,256,256]{4,3,0,1,2:T(8,128)(2,1)S(1)} %get-tuple-element.22), channel_id=1, source_target_pairs={{0,1},{1,2},{2,3},{3,4},{4,5},{5,6},{6,7},{7,8},{8,9},{9,10},{10,1... | collective-permute-start | bytes 3145736 | tf_op jit(solution)/shard_map/ppermute | solution.py:16
  336.6 16.1 %collective-permute-start.3 = (bf16[4,2,1,256,256]{4,3,0,1,2:T(8,128)(2,1)S(1)}, bf16[4,2,1,256,256]{4,3,0,1,2:T(8,128)(2,1)S(1)}, u32[]{:S(2)}, u32[]{:S(2)}) collective-permute-start(bf16[4,2,1,256,256]{4,3,0,1,2:T(8,128)(2,1)S(1)} %get-tuple-element.23), channel_id=1, source_target_pairs={{1,0},{2,1},{3,2},{4,3},{5,4},{6,5},{7,6},{8,7},{9,8},{10,9},{11,1... | collective-permute-start | bytes 3145736 | tf_op jit(solution)/shard_map/ppermute | solution.py:17
  355.2 468.9 %all-gather.11.cloned.1.call-start = ((), (), s32[]{:S(2)}) async-start(), calls=%async_computation.2 | async-start | bytes 9437184 | tf_op jit(solution)/shard_map/all_gather | solution.py:48
  516.1 131.5 %copy-start.1 = (f32[2,2,256,256]{2,3,0,1:T(8,128)S(1)}, f32[2,2,256,256]{2,3,0,1:T(8,128)}, u32[]{:S(2)}) copy-start(f32[2,2,256,256]{2,3,0,1:T(8,128)} %get-tuple-element.15) | copy-start | bytes 3145732
  714.6 1.0 copy-start.2
  715.5 18.4 %copy-start.5 = (f32[2,256,256]{1,2,0:T(8,128)S(1)}, f32[2,256,256]{1,2,0:T(8,128)}, u32[]{:S(2)}) copy-start(f32[2,256,256]{1,2,0:T(8,128)} %copy-done.3) | copy-start | bytes 1572868
  715.5 18.4 %copy-start.8 = (bf16[4,2,256,256]{3,2,1,0:T(8,128)(2,1)S(1)}, bf16[4,2,256,256]{3,2,1,0:T(8,128)(2,1)}, u32[]{:S(2)}) copy-start(bf16[4,2,256,256]{3,2,1,0:T(8,128)(2,1)} %param.7) | copy-start | bytes 3145732
  715.7 13.8 %collective-permute-start.4 = (bf16[4,2,1,256,256]{4,3,0,1,2:T(8,128)(2,1)S(1)}, bf16[4,2,1,256,256]{4,3,0,1,2:T(8,128)(2,1)S(1)}, u32[]{:S(2)}, u32[]{:S(2)}) collective-permute-start(bf16[4,2,1,256,256]{4,3,0,1,2:T(8,128)(2,1)S(1)} %get-tuple-element.20), channel_id=1, source_target_pairs={{0,1},{1,2},{2,3},{3,4},{4,5},{5,6},{6,7},{7,8},{8,9},{9,10},{10,1... | collective-permute-start | bytes 3145736 | tf_op jit(solution)/shard_map/ppermute | solution.py:16
  717.8 16.1 %collective-permute-start.5 = (bf16[4,2,1,256,256]{4,3,0,1,2:T(8,128)(2,1)S(1)}, bf16[4,2,1,256,256]{4,3,0,1,2:T(8,128)(2,1)S(1)}, u32[]{:S(2)}, u32[]{:S(2)}) collective-permute-start(bf16[4,2,1,256,256]{4,3,0,1,2:T(8,128)(2,1)S(1)} %get-tuple-element.21), channel_id=1, source_target_pairs={{1,0},{2,1},{3,2},{4,3},{5,4},{6,5},{7,6},{8,7},{9,8},{10,9},{11,1... | collective-permute-start | bytes 3145736 | tf_op jit(solution)/shard_map/ppermute | solution.py:17
Sparse Core Ops, SparseCore 0:
  34.1 97.9 all-gather.6
  355.3 87.5 all-gather.8
  736.4 87.5 all-gather.10
